TPU v7x, 512 devices: a whole 4x4x16 slice. The times are simulated.
512 devices in a mesh: mp: 64 (over x, z), replica: 8 (over y, core).
Axes of the slice: x: 4, y: 4, z: 16, core: 2. Of those that a mesh axis runs over, the one named last changes fastest.
Arguments:
- pooled_grads: bfloat16 [64, 8, 128, 64, 128], P('mp', 'replica'), may hold values from -0.119628906 to 0.119628906
- table: float32 [64, 512, 128], P('mp'), may hold values from -3 to 3
- state: float32 [64, 512], P('mp'), may hold values from 0.2 to 5
- tile_mult: bfloat16 [64, 8, 64, 128, 128], P('mp', 'replica'), may hold values from 0 to 3, as said below
- tile_rows: int32 [64, 8, 64], P('mp', 'replica'), may hold values from 0 to 3
Outputs:
- new_table: float32 [64, 512, 128], P('mp')
- new_state: float32 [64, 512], P('mp')
Inputs may be any that keep to these rules, and one draw needn't show every extreme that they name: tile_mult holds whole numbers.
All inputs are finite; a program needn't handle non-finite values.
Results may differ from a plain program's by a relative error of at most 0.0003.
Values may be sent and summed in bfloat16 or wider, within the bound.
No kernel may reach another device: no remote copies, remote signals or barrier semaphores. Data moves between devices by JAX's collectives and lax.ppermute only.
A program may use at most 64 MiB of HBM per device.

v0:
```python
import jax
import jax.numpy as jnp
from jax import lax
from jax.sharding import PartitionSpec as P

LEARN_RATE = 0.5
EPSILON = 1e-06


def adagrad(weights_in, accum_in, gradient):
    accum_out = accum_in + jnp.mean(gradient * gradient, axis=-1)
    weights_out = weights_in - LEARN_RATE * gradient / (jnp.sqrt(accum_out)[..., None] + EPSILON)
    return (weights_out, accum_out)


def on_device(pooled_grads, table, state, tile_mult, tile_rows):
    local_grads = pooled_grads[0, 0]
    width = local_grads.shape[-1]
    received = lax.all_to_all(local_grads, "mp", split_axis=1, concat_axis=0, tiled=True)
    counts_bf = tile_mult[0, 0]
    block_size = counts_bf.shape[-1]
    sample_blocks = received.reshape(-1, block_size, width)
    row_ids = tile_rows[0, 0]
    contrib = jnp.einsum(
        "tsr,tse->tre", counts_bf, sample_blocks, preferred_element_type=jnp.float32
    )
    weights_in = table[0]
    accum_in = state[0]
    row_count = weights_in.shape[0]
    row_blocks = row_count // block_size
    onehot = (row_ids[:, None] == jnp.arange(row_blocks, dtype=jnp.int32)[None, :]).astype(
        jnp.float32
    )
    partial_grad = jnp.einsum(
        "tb,tre->bre", onehot, contrib, precision=lax.Precision.HIGHEST
    ).reshape(row_count, width)
    total_grad = lax.psum(partial_grad, "replica")
    weights_out, accum_out = adagrad(weights_in, accum_in, total_grad)
    return (weights_out[None], accum_out[None])


def solution(mesh):
    placed = (
        P("mp", "replica", None, None, None),
        P("mp", None, None),
        P("mp", None),
        P("mp", "replica", None, None, None),
        P("mp", "replica", None),
    )
    return jax.shard_map(
        on_device,
        mesh=mesh,
        in_specs=placed,
        out_specs=(P("mp", None, None), P("mp", None)),
        check_vma=False,
    )
```

profile of v0, /device:TPU:2, one launch (start us, length us, event | category | flops | bytes accessed | tf_op | source)
XLA Modules:
  0.0 211.9 jit_solution(7404038184944069721)
XLA Ops:
  7.2 0.0 copy-start
  7.2 0.0 all-reduce.2.cloned.1.call-start
  7.2 3.1 %copy.16 = bf16[1,1,128,64,128]{4,2,3,1,0:T(8,128)(2,1)S(1)} copy(bf16[1,1,128,64,128]{4,3,2,1,0:T(8,128)(2,1)} %param.5) | data formatting | bytes 4194304 | tf_op args[0]
  10.3 115.6 %all_to_all.15 = bf16[128,64,128]{2,0,1:T(8,128)(2,1)S(1)} all-to-all(bf16[128,64,128]{2,0,1:T(8,128)(2,1)S(1)} %bitcast.26), channel_id=1, replica_groups=mesh['mp'=64,'replica'=8] {'mp'}, dimensions={1} | all-to-all | bytes 4194304 | tf_op jit(solution)/shard_map/all_to_all | solution.py:19
  125.9 0.0 copy-done
  125.9 0.0 copy-start.3
  126.0 0.9 fusion.2
  126.8 0.0 copy-done.3
  126.8 0.0 copy-start.2
  126.9 0.0 copy-start.1
  126.9 3.8 %fusion = f32[4,128,128]{2,0,1:T(4,128)S(1)} fusion(f32[64,128,128]{2,1,0:T(8,128)S(1)} %fusion.2, s32[64]{0:T(128)S(1)} %bitcast.30), kind=kOutput, calls=%fused_computation | convolution fusion | flops 50331904 | bytes 4456704 | tf_op jit(solution)/shard_map/tb,tre->bre/dot_general | solution.py:34
  130.7 0.7 copy.11
  131.4 0.0 all-reduce.2.cloned.1.call-update
  131.4 70.1 %all-reduce.2.cloned.1.call-done = f32[512,128]{1,0:T(8,128)} async-done(((f32[512,128]{1,0:T(8,128)}), f32[512,128]{1,0:T(8,128)}) %all-reduce.2.cloned.1.call-update) | async-done | bytes 262160 | tf_op jit(solution)/shard_map/psum | solution.py:37
  201.5 1.1 multiply_reduce_fusion
  202.6 0.0 copy-done.2
  202.6 0.6 add.26
  203.2 0.0 copy-done.1
  203.2 1.8 fusion.5
  (1 shorter events, 0.0 us)
Async XLA Ops:
  7.2 118.8 %copy-start = (bf16[1,1,64,128,128]{4,3,2,1,0:T(8,128)(2,1)S(1)}, bf16[1,1,64,128,128]{4,3,2,1,0:T(8,128)(2,1)}, u32[]{:S(2)}) copy-start(bf16[1,1,64,128,128]{4,3,2,1,0:T(8,128)(2,1)} %param.8) | copy-start | bytes 6291460
  7.2 194.3 %all-reduce.2.cloned.1.call-start = ((), (), s32[]{:S(2)}) async-start(), calls=%async_computation.1 | async-start | bytes 524288 | tf_op jit(solution)/shard_map/psum | solution.py:37
  125.9 0.9 copy-start.3
  126.8 75.8 %copy-start.2 = (f32[1,512]{1,0:T(1,128)S(1)}, f32[1,512]{1,0:T(1,128)}, u32[]{:S(2)}) copy-start(f32[1,512]{1,0:T(1,128)} %param.7) | copy-start | bytes 6148
  126.9 76.4 %copy-start.1 = (f32[1,512,128]{2,1,0:T(8,128)S(1)}, f32[1,512,128]{2,1,0:T(8,128)}, u32[]{:S(2)}) copy-start(f32[1,512,128]{2,1,0:T(8,128)} %param.6) | copy-start | bytes 786436
Sparse Core Ops, SparseCore 0:
  131.5 69.9 all-reduce.1
where the time goes:
time: 212 us
  blocking collectives  116 us (55%)
  waiting for transfers between devices  70.1 us (33%)
  between operations  14.1 us (7%)
  matrix products  4.67 us (2%)
  local copies, waits for them, and re-layouts  3.83 us (2%)
  other arithmetic  3.48 us (2%)
    all_to_all x1, blocking collectives, on_device(): lax.all_to_all(local_grads, 'mp', split_axis=1, concat_axis=0, tiled=True)  116 us
    psum x1, waiting for transfers between devices, on_device(): total_grad = lax.psum(partial_grad, 'replica')  70.1 us
  transfers between devices with their start and end apart: 1, of which 1 were waited for; matrix products, arithmetic and copies ran while one was open for 0% of the time, Pallas kernels for 0%

commit v1 on v0

--- a/solution.py
+++ b/solution.py
@@ -34,7 +34,7 @@
     partial_grad = jnp.einsum(
         "tb,tre->bre", onehot, contrib, precision=lax.Precision.HIGHEST
     ).reshape(row_count, width)
-    total_grad = lax.psum(partial_grad, "replica")
+    total_grad = jnp.sum(lax.all_gather(partial_grad, "replica"), axis=0)
     weights_out, accum_out = adagrad(weights_in, accum_in, total_grad)
     return (weights_out[None], accum_out[None])
 

time: 212 us -> 170 us (0.80)
  the two profiles are of different devices: /device:TPU:2 before, /device:TPU:1 now
where the time goes in v1:
time: 170 us
  blocking collectives  114 us (67%)
  waiting for transfers between devices  30.7 us (18%)
  between operations  14.1 us (8%)
  matrix products  4.67 us (3%)
  local copies, waits for them, and re-layouts  3.83 us (2%)
  other arithmetic  3.3 us (2%)
    all_to_all x1, blocking collectives, on_device(): lax.all_to_all(local_grads, 'mp', split_axis=1, concat_axis=0, tiled=True)  114 us
    all_gather x1, waiting for transfers between devices, on_device(): total_grad = jnp.sum(lax.all_gather(partial_grad, 'replica'), axis=0)  30.7 us
    dot_general x1, matrix products, on_device(): jnp.einsum('tb,tre->bre', onehot, contrib, precision=lax.Precision.HIGHEST)  3.8 us
  transfers between devices with their start and end apart: 1, of which 1 were waited for; matrix products, arithmetic and copies ran while one was open for 0% of the time, Pallas kernels for 0%

profile of v1, /device:TPU:1, one launch (start us, length us, event | category | flops | bytes accessed | tf_op | source)
XLA Modules:
  0.0 170.2 jit_solution(7320788965687708744)
XLA Ops:
  7.2 0.0 copy-start
  7.2 0.0 all-gather.2.cloned.1.call-start
  7.2 3.1 %copy.16 = bf16[1,1,128,64,128]{4,2,3,1,0:T(8,128)(2,1)S(1)} copy(bf16[1,1,128,64,128]{4,3,2,1,0:T(8,128)(2,1)} %param.5) | data formatting | bytes 4194304 | tf_op args[0]
  10.3 113.6 %all_to_all.15 = bf16[128,64,128]{2,0,1:T(8,128)(2,1)S(1)} all-to-all(bf16[128,64,128]{2,0,1:T(8,128)(2,1)S(1)} %bitcast.24), channel_id=1, replica_groups=mesh['mp'=64,'replica'=8] {'mp'}, dimensions={1} | all-to-all | bytes 4194304 | tf_op jit(solution)/shard_map/all_to_all | solution.py:19
  123.9 0.0 copy-done
  123.9 0.0 copy-start.3
  123.9 0.9 fusion.2
  124.8 0.0 copy-done.3
  124.8 3.8 %fusion = f32[4,128,128]{2,0,1:T(4,128)S(1)} fusion(f32[64,128,128]{2,1,0:T(8,128)S(1)} %fusion.2, s32[64]{0:T(128)S(1)} %bitcast.28), kind=kOutput, calls=%fused_computation | convolution fusion | flops 50331904 | bytes 4456704 | tf_op jit(solution)/shard_map/tb,tre->bre/dot_general | solution.py:34
  128.6 0.0 copy-start.2
  128.6 0.0 copy-start.1
  128.6 0.7 copy.11
  129.3 0.0 all-gather.2.cloned.1.call-update
  129.3 30.7 %all-gather.2.cloned.1.call-done = f32[8,512,128]{2,1,0:T(8,128)} async-done(((f32[1,512,128]{2,1,0:T(8,128)}), f32[8,512,128]{2,1,0:T(8,128)}) %all-gather.2.cloned.1.call-update) | async-done | bytes 2097168 | tf_op jit(solution)/shard_map/all_gather | solution.py:37
  160.0 1.7 %reduce_sum.18 = f32[512,128]{1,0:T(8,128)S(1)} reduce(f32[8,512,128]{2,1,0:T(8,128)} %all-gather.2.cloned.1.call-done, f32[]{:T(128)} %constant.1.clone.1), dimensions={0}, to_apply=%region_0.0 | reduce | flops 458752 | bytes 2359300 | tf_op jit(solution)/shard_map/reduce_sum | solution.py:37
  161.7 0.1 multiply_reduce_fusion
  161.9 0.0 copy-done.2
  161.9 0.6 add.24
  162.5 0.0 copy-done.1
  162.5 0.8 fusion.5
  (1 shorter events, 0.0 us)
Async XLA Ops:
  7.2 116.7 %copy-start = (bf16[1,1,64,128,128]{4,3,2,1,0:T(8,128)(2,1)S(1)}, bf16[1,1,64,128,128]{4,3,2,1,0:T(8,128)(2,1)}, u32[]{:S(2)}) copy-start(bf16[1,1,64,128,128]{4,3,2,1,0:T(8,128)(2,1)} %param.8) | copy-start | bytes 6291460
  7.2 152.8 %all-gather.2.cloned.1.call-start = ((), (), s32[]{:S(2)}) async-start(), calls=%async_computation.1 | async-start | bytes 2359296 | tf_op jit(solution)/shard_map/all_gather | solution.py:37
  123.9 0.9 copy-start.3
  128.6 33.3 %copy-start.2 = (f32[1,512]{1,0:T(1,128)S(1)}, f32[1,512]{1,0:T(1,128)}, u32[]{:S(2)}) copy-start(f32[1,512]{1,0:T(1,128)} %param.7) | copy-start | bytes 6148
  128.6 33.9 %copy-start.1 = (f32[1,512,128]{2,1,0:T(8,128)S(1)}, f32[1,512,128]{2,1,0:T(8,128)}, u32[]{:S(2)}) copy-start(f32[1,512,128]{2,1,0:T(8,128)} %param.6) | copy-start | bytes 786436
Sparse Core Ops, SparseCore 0:
  129.5 30.5 all-gather.1
